TPU v7x, 32 devices: a whole 2x2x4 slice. The times are simulated.
32 devices in a mesh: gx: 4 (over z), gy: 4 (over y, x), gz: 2 (over core).
Axes of the slice: x: 2, y: 2, z: 4, core: 2. Of those that a mesh axis runs over, the one named last changes fastest.
Arguments:
- species_field: float32 [8, 384, 6144], P('gz', 'gx', 'gy'), may hold values from -24 to 24
- start_first: float32 [384, 96], replicated, may hold values from -0.3125 to 0.3125
- start_second: float32 [384, 96], replicated, may hold values from -0.3125 to 0.3125
Outputs:
- factor_first: float32 [384, 96], replicated
- factor_second: float32 [384, 96], replicated
- core_tensor: float32 [16, 8, 96, 96], P('gx', 'gz', 'gy')
All inputs are finite; a program needn't handle non-finite values.
Results may differ from a plain program's by a relative error of at most 0.0003.
Values sent between devices are 32-bit elements; how exact they have to be, the bound alone decides.
A program may use at most 64 MiB of HBM per device.

v0:
```python
import jax
import jax.numpy as jnp
from jax import lax
from jax.sharding import PartitionSpec as P

S = 16
ITERS = 2


exact_precision = lax.Precision.HIGHEST


def leading(image_fn, start):
    current = start
    for turn in range(ITERS):
        images = image_fn(current)
        cross_gram = jnp.dot(images.T, images, precision=exact_precision)
        lower_factor = jnp.linalg.cholesky(cross_gram)
        current = lax.linalg.triangular_solve(
            lower_factor, images, left_side=False, lower=True, transpose_a=True
        )
    return current


def local(species_field, start_first, start_second):
    fibres = lax.all_to_all(species_field, "gx", split_axis=2, concat_axis=1, tiled=True)
    partial_gram = jnp.einsum("zic,zjc->ij", fibres, fibres, precision=exact_precision)
    gram_first = lax.psum(partial_gram, ("gx", "gy", "gz"))

    def image_first(current):
        return jnp.dot(gram_first, current, precision=exact_precision)

    factor_first = leading(image_first, start_first)
    cells = fibres.shape[2] // S
    blocks = fibres.reshape(fibres.shape[0], fibres.shape[1], cells, S)
    projected = jnp.einsum("ziks,ir->zrsk", blocks, factor_first, precision=exact_precision)
    rows_second = lax.all_to_all(
        lax.all_to_all(projected, "gx", split_axis=2, concat_axis=3, tiled=True),
        "gy",
        split_axis=1,
        concat_axis=3,
        tiled=True,
    )
    flat_rows = rows_second.reshape(-1, rows_second.shape[3])
    partial_second = jnp.dot(flat_rows.T, flat_rows, precision=exact_precision)
    gram_second = lax.psum(partial_second, ("gx", "gy", "gz"))

    def image_second(current):
        return jnp.dot(gram_second, current, precision=exact_precision)

    factor_second = leading(image_second, start_second)
    core_local = jnp.einsum("zrsj,jq->szrq", rows_second, factor_second, precision=exact_precision)
    return (factor_first, factor_second, core_local)


def solution(mesh):
    return jax.shard_map(
        local,
        mesh=mesh,
        in_specs=(P("gz", "gx", "gy"), P(), P()),
        out_specs=(P(), P(), P("gx", "gz", "gy", None)),
        check_vma=False,
    )
```

profile of v0, /device:TPU:0, one launch (start us, length us, event | category | flops | bytes accessed | tf_op | source)
XLA Modules:
  0.0 482.7 jit_solution(708190136586059608)
XLA Ops:
  7.2 0.0 copy-start
  7.2 0.0 all-reduce.3.cloned.1.call-start
  7.2 4.5 copy.38
  11.8 77.0 %all_to_all.54 = f32[4,96,1536]{1,0,2:T(4,128)S(1)} all-to-all(f32[4,96,1536]{1,0,2:T(4,128)} %copy.38), channel_id=1, replica_groups=mesh['gx'=4,'gy'=4,'gz'=2] {'gx'}, dimensions={2} | all-to-all | bytes 4718592 | tf_op jit(solution)/shard_map/all_to_all | solution.py:26
  88.8 2.8 copy.40
  91.5 7.1 %convolution_bitcast_fusion = f32[384,384]{1,0:T(8,128)} fusion(f32[4,384,384]{2,1,0:T(8,128)} %bitcast.105), kind=kOutput, calls=%fused_computation.4 | convolution fusion | flops 2717908992 | bytes 2949120 | tf_op jit(solution)/shard_map/zic,zjc->ij/dot_general | solution.py:27
  98.7 0.0 all-reduce.3.cloned.1.call-update
  98.7 0.0 all-reduce.5.cloned.1.call-start
  98.7 3.7 copy.63
  102.4 3.6 reshape.25
  106.0 120.4 %all-reduce.3.cloned.1.call-done = f32[384,384]{1,0:T(8,128)} async-done(((f32[384,384]{1,0:T(8,128)}), f32[384,384]{1,0:T(8,128)}) %all-reduce.3.cloned.1.call-update) | async-done | bytes 589840 | tf_op jit(solution)/shard_map/psum | solution.py:28
  226.4 1.9 fusion.23
  228.2 0.3 fusion.24
  228.6 0.1 copy.41
  228.7 8.8 %cholesky.74 = f32[96,96]{1,0:T(8,128)S(1)} custom-call(f32[96,96]{1,0:T(8,128)S(1)} %fusion.20), custom_call_target="Cholesky" | custom-call | tf_op jit(solution)/shard_map/jit(cholesky)/cholesky | solution.py:18
  237.5 0.6 compare_reduce_fusion.3
  238.1 0.7 fusion.7
  238.8 7.4 %custom-call.8 = f32[1,96,96]{1,2,0:T(8,128)S(1)} custom-call(f32[1,96,96]{2,1,0:T(8,128)S(1)} %fusion.7), custom_call_target="InvertDiagBlocksLowerTriangular" | custom-call | tf_op jit(solution)/shard_map/triangular_solve/custom-call.0 | solution.py:19
  246.2 0.3 convolution_bitcast_fusion.3
  246.5 0.0 copy-done.1
  246.5 0.7 fusion.25
  247.2 0.3 fusion.26
  247.6 0.1 copy.42
  247.7 8.8 %cholesky.85 = f32[96,96]{1,0:T(8,128)S(1)} custom-call(f32[96,96]{1,0:T(8,128)S(1)} %fusion.18), custom_call_target="Cholesky" | custom-call | tf_op jit(solution)/shard_map/jit(cholesky)/cholesky | solution.py:18
  256.5 0.6 compare_reduce_fusion.2
  257.2 0.7 fusion.8
  257.8 7.4 %custom-call.9 = f32[1,96,96]{1,2,0:T(8,128)S(1)} custom-call(f32[1,96,96]{2,1,0:T(8,128)S(1)} %fusion.8), custom_call_target="InvertDiagBlocksLowerTriangular" | custom-call | tf_op jit(solution)/shard_map/triangular_solve/custom-call.0 | solution.py:19
  265.2 0.3 fusion.16
  265.5 0.0 copy-start.3
  265.5 2.6 fusion.2
  268.2 0.1 copy.44
  268.3 23.2 %all_to_all.55 = f32[4,96,16,24]{1,3,0,2:T(8,128)S(1)} all-to-all(f32[4,96,16,24]{1,3,0,2:T(8,128)S(1)} %copy.44), channel_id=1, replica_groups=mesh['gx'=4,'gy'=4,'gz'=2] {'gx'}, dimensions={2} | all-to-all | bytes 1179648 | tf_op jit(solution)/shard_map/all_to_all | solution.py:38
  291.5 0.1 copy.46
  291.6 0.5 copy.47
  292.1 13.3 %all_to_all.56 = f32[4,96,4,96]{3,2,0,1:T(4,128)S(1)} all-to-all(f32[4,96,4,96]{3,2,0,1:T(4,128)S(1)} %copy.47), channel_id=1, replica_groups=mesh['gx'=4,'gy'=4,'gz'=2] {'gy'}, dimensions={1} | all-to-all | bytes 1179648 | tf_op jit(solution)/shard_map/all_to_all | solution.py:37
  305.4 0.3 copy.48
  305.6 0.2 copy.49
  305.8 0.4 reshape.26
  306.2 0.0 copy-start.5
  306.3 2.1 fusion.27
  308.4 0.0 all-reduce.5.cloned.1.call-update
  308.4 0.2 copy.52
  308.6 0.4 all_to_all.50
  309.0 126.3 %all-reduce.5.cloned.1.call-done = f32[384,384]{1,0:T(8,128)} async-done(((f32[384,384]{1,0:T(8,128)}), f32[384,384]{1,0:T(8,128)}) %all-reduce.5.cloned.1.call-update) | async-done | bytes 589840 | tf_op jit(solution)/shard_map/psum | solution.py:46
  435.3 1.9 fusion.28
  437.2 0.3 fusion.29
  437.5 0.1 copy.50
  437.6 8.8 %cholesky.96 = f32[96,96]{1,0:T(8,128)S(1)} custom-call(f32[96,96]{1,0:T(8,128)S(1)} %fusion.15), custom_call_target="Cholesky" | custom-call | tf_op jit(solution)/shard_map/jit(cholesky)/cholesky | solution.py:18
  446.4 0.6 compare_reduce_fusion.1
  447.1 0.7 fusion.9
  447.7 7.4 %custom-call.10 = f32[1,96,96]{1,2,0:T(8,128)S(1)} custom-call(f32[1,96,96]{2,1,0:T(8,128)S(1)} %fusion.9), custom_call_target="InvertDiagBlocksLowerTriangular" | custom-call | tf_op jit(solution)/shard_map/triangular_solve/custom-call.0 | solution.py:19
  455.1 0.3 convolution_bitcast_fusion.2
  455.4 0.0 copy-done.2
  455.5 0.7 fusion.30
  456.2 0.3 fusion.31
  456.5 0.1 copy.51
  456.6 8.8 %cholesky.107 = f32[96,96]{1,0:T(8,128)S(1)} custom-call(f32[96,96]{1,0:T(8,128)S(1)} %fusion.13), custom_call_target="Cholesky" | custom-call | tf_op jit(solution)/shard_map/jit(cholesky)/cholesky | solution.py:18
  465.5 0.6 compare_reduce_fusion
  466.1 0.7 fusion.10
  466.8 7.4 %custom-call.11 = f32[1,96,96]{1,2,0:T(8,128)S(1)} custom-call(f32[1,96,96]{2,1,0:T(8,128)S(1)} %fusion.10), custom_call_target="InvertDiagBlocksLowerTriangular" | custom-call | tf_op jit(solution)/shard_map/triangular_solve/custom-call.0 | solution.py:19
  474.1 0.3 fusion.11
  474.5 0.0 copy-start.4
  474.5 0.6 convolution_bitcast_fusion.1
  475.1 0.7 copy.53
  (14 shorter events, 0.2 us)
Async XLA Ops:
  7.2 219.2 %copy-start = (f32[384,96]{0,1:T(8,128)S(1)}, f32[384,96]{0,1:T(8,128)}, u32[]{:S(2)}) copy-start(f32[384,96]{0,1:T(8,128)} %param.7) | copy-start | bytes 442372
  7.2 219.2 %all-reduce.3.cloned.1.call-start = ((), (), s32[]{:S(2)}) async-start(), calls=%async_computation.3 | async-start | bytes 1179648 | tf_op jit(solution)/shard_map/psum | solution.py:28
  98.7 336.6 %all-reduce.5.cloned.1.call-start = ((), (), s32[]{:S(2)}) async-start(), calls=%async_computation.4 | async-start | bytes 1179648 | tf_op jit(solution)/shard_map/psum | solution.py:46
  226.4 20.1 %copy-start.1 = (f32[384,384]{1,0:T(8,128)S(1)}, f32[384,384]{1,0:T(8,128)}, u32[]{:S(2)}) copy-start(f32[384,384]{1,0:T(8,128)} %all-reduce.3.cloned.1.call-done) | copy-start | bytes 1769476
  265.5 2.8 copy-start.3
  306.2 129.1 %copy-start.5 = (f32[384,96]{0,1:T(8,128)S(1)}, f32[384,96]{0,1:T(8,128)}, u32[]{:S(2)}) copy-start(f32[384,96]{0,1:T(8,128)} %param.8) | copy-start | bytes 442372
  435.3 20.1 %copy-start.2 = (f32[384,384]{1,0:T(8,128)S(1)}, f32[384,384]{1,0:T(8,128)}, u32[]{:S(2)}) copy-start(f32[384,384]{1,0:T(8,128)} %all-reduce.5.cloned.1.call-done) | copy-start | bytes 1769476
  474.5 1.3 copy-start.4
Sparse Core Ops, SparseCore 0:
  98.8 127.5 all-reduce.2
  308.5 126.7 all-reduce.4
where the time goes:
time: 483 us
  waiting for transfers between devices  247 us (51%)
  blocking collectives  114 us (24%)
  other arithmetic  69.9 us (14%)
  matrix products  20.4 us (4%)
  local copies, waits for them, and re-layouts  17.7 us (4%)
  between operations  14.4 us (3%)
    psum x1, waiting for transfers between devices, local(): gram_second = lax.psum(partial_second, ('gx', 'gy', 'gz'))  126 us
    psum x1, waiting for transfers between devices, local(): gram_first = lax.psum(partial_gram, ('gx', 'gy', 'gz'))  120 us
    all_to_all x1, blocking collectives, local(): lax.all_to_all(species_field, 'gx', split_axis=2, concat_axis=1, tiled=True)  77 us
    another operation x12, other arithmetic, leading(): lower_factor = jnp.linalg.cholesky(cross_gram)  37.8 us
    another operation x8, other arithmetic, leading(): lax.linalg.triangular_solve(lower_factor, images, left_side=False, lower=...  32 us
    all_to_all x1, blocking collectives, local(): lax.all_to_all(projected, 'gx', split_axis=2, concat_axis=3, tiled=True)  23.2 us
    all_to_all x1, blocking collectives, local(): lax.all_to_all(lax.all_to_all(projected, 'gx', split_axis=2, concat_axis=...  13.3 us
  transfers between devices with their start and end apart: 2, of which 2 were waited for; matrix products, arithmetic and copies ran while one was open for 2% of the time, Pallas kernels for 0%

commit v1 on v0

v1 whole, which is shorter than its diff:
```python
import functools

import jax
import jax.numpy as jnp
from jax import lax
from jax.experimental import pallas as pl
from jax.experimental.pallas import tpu as pltpu
from jax.sharding import PartitionSpec as P

S = 16
ITERS = 2
PANEL = 16
MESH = pl.DeviceIdType.MESH
VMEM = pl.BlockSpec(memory_space=pltpu.VMEM)

exact_precision = lax.Precision.HIGHEST


def dot_dims(a, b, contract_a, contract_b):
    return lax.dot_general(
        a, b, (((contract_a,), (contract_b,)), ((), ())),
        precision=exact_precision, preferred_element_type=jnp.float32,
    )


def partners(n, me):
    if n == 4:
        return [3 - me, lax.rem(me + 2, 4), me + 1 - 2 * lax.rem(me, 2)]
    return [lax.rem(me + d, n) for d in range(1, n)]


def send(src, dst, send_sem, recv_sem, target):
    copy = pltpu.make_async_remote_copy(
        src_ref=src, dst_ref=dst, send_sem=send_sem, recv_sem=recv_sem,
        device_id=target, device_id_type=MESH,
    )
    copy.start()
    return copy


def greet(targets):
    barrier = pltpu.get_barrier_semaphore()
    for target in targets:
        pl.semaphore_signal(barrier, inc=1, device_id=target, device_id_type=MESH)
    pl.semaphore_wait(barrier, len(targets))


def all_reduce_kernel(axes, sizes, splits, x_ref, o_ref, *scratch):
    levels = len(axes)
    landing, totals = scratch[:levels], scratch[levels : 2 * levels - 1]
    send_sems, recv_sems = scratch[2 * levels - 1 :]
    me = [lax.axis_index(axis) for axis in axes]
    peers = [partners(n, m) for n, m in zip(sizes, me)]
    greet([{axis: p} for axis, ps in zip(axes, peers) for p in ps])

    spot = [m if split > 1 else 0 for m, split in zip(me, splits)]
    sem = 0
    held = x_ref
    for level in range(levels):
        axis, n, split = axes[level], sizes[level], splits[level]
        land = landing[level]
        copies = []
        for p in peers[level]:
            src = held.at[p] if split > 1 else held.at[0]
            copies.append(send(src, land.at[me[level]], send_sems.at[sem], recv_sems.at[sem], {axis: p}))
            sem += 1
        land[me[level]] = held[spot[level]]
        for copy in copies:
            copy.wait()
        total = land[0]
        for source in range(1, n):
            total = total + land[source]
        if level < levels - 1:
            totals[level][...] = total
            held = totals[level]
        else:
            o_ref[tuple(spot)] = total

    for level in reversed(range(levels)):
        if splits[level] == 1:
            continue
        block = o_ref.at[tuple(spot[: level + 1])]
        copies = []
        for p in peers[level]:
            copies.append(send(block, block, send_sems.at[sem], recv_sems.at[sem], {axes[level]: p}))
            sem += 1
        for copy in copies:
            copy.wait()


def all_reduce(x, axes, sizes, collective_id):
    rows, columns = x.shape
    splits = []
    for n in sizes:
        splits.append(n if rows % n == 0 else 1)
        rows //= splits[-1]
    blocked = x.reshape(*splits, rows, columns)
    landing = [
        pltpu.VMEM((n, *splits[level + 1 :], rows, columns), jnp.float32)
        for level, n in enumerate(sizes)
    ]
    totals = [pltpu.VMEM((*splits[level + 1 :], rows, columns), jnp.float32) for level in range(len(sizes) - 1)]
    count = sum(n - 1 for n in sizes) + sum(n - 1 for n, split in zip(sizes, splits) if split > 1)
    out = pl.pallas_call(
        functools.partial(all_reduce_kernel, axes, sizes, splits),
        out_shape=jax.ShapeDtypeStruct(blocked.shape, jnp.float32),
        in_specs=[VMEM],
        out_specs=VMEM,
        scratch_shapes=landing + totals + [pltpu.SemaphoreType.DMA((count,)), pltpu.SemaphoreType.DMA((count,))],
        compiler_params=pltpu.CompilerParams(collective_id=collective_id, has_side_effects=True),
    )(blocked)
    return out.reshape(x.shape)


def fibres_kernel(n, x_ref, o_ref, send_sems, recv_sems):
    me = lax.axis_index("gx")
    depth, rows, width = x_ref.shape[0], x_ref.shape[1], o_ref.shape[-1]
    peers = partners(n, me)
    greet([{"gx": p} for p in peers])
    copies = []
    for turn, p in enumerate(peers):
        columns = pl.ds(pl.multiple_of(p * width, width), width)
        copies.append(
            send(x_ref.at[:, :, columns], o_ref.at[:, me], send_sems.at[turn], recv_sems.at[turn], {"gx": p})
        )
    own = pl.ds(pl.multiple_of(me * width, width), width)
    for level in range(depth):
        o_ref[level, me] = x_ref[level, :, own]
    for copy in copies:
        copy.wait()


def gather_fibres(field, n):
    depth, rows, columns = field.shape
    width = columns // n
    if width % 128:
        return lax.all_to_all(field, "gx", split_axis=2, concat_axis=1, tiled=True)
    out = pl.pallas_call(
        functools.partial(fibres_kernel, n),
        out_shape=jax.ShapeDtypeStruct((depth, n, rows, width), jnp.float32),
        in_specs=[VMEM],
        out_specs=VMEM,
        scratch_shapes=[pltpu.SemaphoreType.DMA((n - 1,)), pltpu.SemaphoreType.DMA((n - 1,))],
        compiler_params=pltpu.CompilerParams(collective_id=0, has_side_effects=True),
    )(field)
    return out.reshape(depth, n * rows, width)


def exchange_kernel(nx, ny, x_ref, o_ref, send_sems, recv_sems):
    mx, my = lax.axis_index("gx"), lax.axis_index("gy")
    peers = [(px, my) for px in partners(nx, mx)]
    for py in partners(ny, my):
        peers += [(px, py) for px in partners(nx, mx) + [mx]]
    greet([{"gx": px, "gy": py} for px, py in peers])
    copies = []
    for turn, (px, py) in enumerate(peers):
        copies.append(
            send(x_ref.at[py, px], o_ref.at[my, mx], send_sems.at[turn], recv_sems.at[turn], {"gx": px, "gy": py})
        )
    o_ref[my, mx] = x_ref[my, mx]
    for copy in copies:
        copy.wait()


def exchange(blocks):
    ny, nx = blocks.shape[:2]
    count = nx * ny - 1
    return pl.pallas_call(
        functools.partial(exchange_kernel, nx, ny),
        out_shape=jax.ShapeDtypeStruct(blocks.shape, jnp.float32),
        in_specs=[VMEM],
        out_specs=VMEM,
        scratch_shapes=[pltpu.SemaphoreType.DMA((count,)), pltpu.SemaphoreType.DMA((count,))],
        compiler_params=pltpu.CompilerParams(collective_id=1, has_side_effects=True),
    )(blocks)


def inverse_lower(cross):
    rank = cross.shape[0]
    panel = PANEL if rank % PANEL == 0 else 8
    row = lax.broadcasted_iota(jnp.int32, (rank, rank), 0)
    column = lax.broadcasted_iota(jnp.int32, (rank, rank), 1)
    rest = cross
    rest_inverse = jnp.where(row == column, 1.0, 0.0).astype(jnp.float32)
    local_row = lax.broadcasted_iota(jnp.int32, (panel, rank), 0)
    done = []
    for start in range(0, rank, panel):
        upper = rest[:panel]
        inverse = rest_inverse[:panel]
        columns = [
            jnp.broadcast_to(upper[:, start + j : start + j + 1], (panel, rank)) for j in range(panel)
        ]
        diagonal = jnp.ones((panel, rank), jnp.float32)
        for j in range(panel):
            pivot = jnp.broadcast_to(columns[j][j : j + 1], (panel, rank))
            diagonal = jnp.where(local_row == j, pivot, diagonal)
            if j == panel - 1:
                break
            factor = jnp.where(local_row > j, columns[j] * (1.0 / pivot), 0.0)
            for other in range(j + 1, panel):
                columns[other] = columns[other] - factor * columns[other][j : j + 1]
            upper = upper - factor * upper[j : j + 1]
            inverse = inverse - factor * inverse[j : j + 1]
        done.append(inverse * (1.0 / jnp.sqrt(diagonal)))
        if start + panel < rank:
            scaled = upper / diagonal
            update = dot_dims(scaled, jnp.concatenate([upper, inverse], axis=1), 0, 0)
            after = start + panel
            rest = rest[panel:] - update[after:, :rank]
            rest_inverse = rest_inverse[panel:] - update[after:, rank:]
    return jnp.concatenate(done, axis=0)


def power_kernel(gram_ref, start_ref, out_ref):
    current = start_ref[...]
    for turn in range(ITERS):
        images = dot_dims(gram_ref[...], current, 1, 0)
        cross = dot_dims(images, images, 0, 0)
        current = dot_dims(images, inverse_lower(cross), 1, 1)
    out_ref[...] = current


def leading(gram, start):
    return pl.pallas_call(
        power_kernel,
        out_shape=jax.ShapeDtypeStruct(start.shape, jnp.float32),
        in_specs=[VMEM, VMEM],
        out_specs=VMEM,
    )(gram, start)


def local(nx, ny, nz, species_field, start_first, start_second):
    axes, sizes = ("gz", "gy", "gx"), (nz, ny, nx)
    fibres = gather_fibres(species_field, nx)
    partial_gram = jnp.einsum("zic,zjc->ij", fibres, fibres, precision=exact_precision)
    gram_first = all_reduce(partial_gram, axes, sizes, 2)
    factor_first = leading(gram_first, start_first)

    depth = fibres.shape[0]
    cells = fibres.shape[2] // S
    rank = start_first.shape[1]
    species, ranks = S // nx, rank // ny
    projected = jnp.einsum("zim,ir->zmr", fibres, factor_first, precision=exact_precision)
    blocks = projected.reshape(depth, cells, nx, species, ny, ranks)
    blocks = blocks.transpose(4, 2, 1, 3, 0, 5).reshape(ny, nx, cells, species * depth * ranks)
    columns = exchange(blocks)
    columns = columns.reshape(ny * nx * cells, species * depth * ranks)
    partial_second = dot_dims(columns, columns, 1, 1)
    gram_second = all_reduce(partial_second, axes, sizes, 3)
    factor_second = leading(gram_second, start_second)
    core = dot_dims(columns, factor_second, 0, 0)
    core = core.reshape(species, depth, ranks, factor_second.shape[1])
    return (factor_first, factor_second, core)


def solution(mesh):
    return jax.shard_map(
        functools.partial(local, mesh.shape["gx"], mesh.shape["gy"], mesh.shape["gz"]),
        mesh=mesh,
        in_specs=(P("gz", "gx", "gy"), P(), P()),
        out_specs=(P(), P(), P("gx", "gz", "gy", None)),
        check_vma=False,
    )
```

time: 483 us -> 197 us (0.41)
  waiting for transfers between devices: 247 us -> 0 us
  Pallas kernels: 0 us -> 156 us
  blocking collectives: 114 us -> 0 us
  other arithmetic: 69.9 us -> 0 us
  between operations: 14.4 us -> 0.72 us
  local copies, waits for them, and re-layouts: 17.7 us -> 25.4 us
  matrix products: 20.4 us -> 14.6 us
    psum x2 -> x0, waiting for transfers between devices: 247 us -> none  [the longest x1 126 us: local(): gram_second = lax.psum(partial_second, ('gx', 'gy', 'gz'))]
    pallas_call x0 -> x6, Pallas kernels: none -> 156 us  [the longest x1 59.6 us: gather_fibres(): pl.pallas_call(functools.partial(fibres_kernel, n), out_shape=jax.ShapeDt...]
    all_to_all x3 -> x0, blocking collectives: 114 us -> none  [the longest x1 77 us: local(): lax.all_to_all(species_field, 'gx', split_axis=2, concat_axis=1, tiled=True)]
    another operation x20 -> x0, other arithmetic: 69.9 us -> none  [the longest x12 37.8 us: leading(): lower_factor = jnp.linalg.cholesky(cross_gram)]
    reshape x2 -> x5, local copies, waits for them, and re-layouts: 3.94 us -> 14.8 us  [the longest x1 4.46 us: local(): blocks.transpose(4, 2, 1, 3, 0, 5)]
    all_to_all x8 -> x0, local copies, waits for them, and re-layouts: 8.06 us -> none  [the longest x2 6.45 us: local(): lax.all_to_all(species_field, 'gx', split_axis=2, concat_axis=1, tiled=True)]
    dot_general x11 -> x3, matrix products: 11.9 us -> 8.52 us  [the longest x2 6.07 us: dot_dims(): lax.dot_general(a, b, (((contract_a,), (contract_b,)), ((), ())), precisi...]
  transfers between devices with their start and end apart: 2 -> 0, of which waited for: 2 -> 0; matrix products, arithmetic and copies ran while one was open for 2% -> 0% of each run, Pallas kernels for 0% -> 0%
where the time goes in v1:
time: 197 us; the launch traced here: 196 us
  Pallas kernels  156 us (79%)
  local copies, waits for them, and re-layouts  25.4 us (13%)
  matrix products  14.6 us (7%)
    pallas_call x1, Pallas kernels, gather_fibres(): pl.pallas_call(functools.partial(fibres_kernel, n), out_shape=jax.ShapeDt...  59.6 us
    pallas_call x2, Pallas kernels, all_reduce(): pl.pallas_call(functools.partial(all_reduce_kernel, axes, sizes, splits),...  53.1 us
    pallas_call x2, Pallas kernels, leading(): pl.pallas_call(power_kernel, out_shape=jax.ShapeDtypeStruct(start.shape,...  23.1 us
    pallas_call x1, Pallas kernels, exchange(): pl.pallas_call(functools.partial(exchange_kernel, nx, ny), out_shape=jax....  19.6 us
    dot_general x2, matrix products, dot_dims(): lax.dot_general(a, b, (((contract_a,), (contract_b,)), ((), ())), precisi...  6.07 us
    dot_general x1, matrix products, local(): jnp.einsum('zic,zjc->ij', fibres, fibres, precision=exact_precision)  6.04 us
    unnamed x12, local copies, waits for them, and re-layouts  5.06 us
    reshape x1, local copies, waits for them, and re-layouts, local(): blocks.transpose(4, 2, 1, 3, 0, 5)  4.46 us

profile of v1, /device:TPU:0, one launch (start us, length us, event | category | flops | bytes accessed | tf_op | source)
XLA Modules:
  0.0 196.2 jit_solution(4053065288133088817)
XLA Ops:
  0.6 59.6 %shard_map.58 = f32[4,4,96,384]{3,2,1,0:T(8,128)} custom-call(f32[4,96,1536]{2,1,0:T(8,128)} %x_ref.1), custom_call_target="tpu_custom_call" | custom-call | tf_op jit(solution)/shard_map/pallas_call | solution.py:138
  60.3 0.0 copy-start
  60.3 3.3 %copy.15 = f32[4,384,384]{2,0,1:T(4,128)S(1)} copy(f32[4,384,384]{2,1,0:T(8,128)} %bitcast.35) | data formatting | bytes 4718592 | tf_op jit(solution)/shard_map/reshape | solution.py:146
  63.6 0.0 copy-done
  63.6 6.0 %fusion.2.x_ref = f32[2,4,4,12,384]{4,3,2,1,0:T(8,128)} fusion(f32[4,384,384,1,1,1]{2,1,0,5,4,3:T(8,128)S(1)} %bitcast.36, f32[2,4,4,12,384,4]{4,5,3,2,1,0:T(4,128)S(1)} %bitcast.38), kind=kOutput, calls=%fused_computation.2 | convolution fusion | flops 2717908992 | bytes 5308416 | tf_op jit(solution)/shard_map/zic,zjc->ij/dot_general | solution.py:235
  69.7 0.0 copy-start.2
  69.7 27.5 %shard_map.59 = f32[2,4,4,12,384]{4,3,2,1,0:T(8,128)} custom-call(f32[2,4,4,12,384]{4,3,2,1,0:T(8,128)} %fusion.2.x_ref), custom_call_target="tpu_custom_call" | custom-call | tf_op jit(solution)/shard_map/pallas_call | solution.py:104
  97.2 2.0 %reshape.32.gram_ref = f32[384,384]{1,0:T(8,128)} reshape(f32[2,4,4,12,384]{4,3,2,1,0:T(8,128)} %shard_map.59) | data formatting | bytes 1179648 | tf_op jit(solution)/shard_map/reshape | solution.py:112
  99.2 0.0 copy-done.2
  99.2 0.8 copy.17.start_ref
  100.0 11.6 %shard_map.60 = f32[384,96]{1,0:T(8,128)} custom-call(f32[384,384]{1,0:T(8,128)} %reshape.32.gram_ref, f32[384,96]{1,0:T(8,128)} %copy.17.start_ref), custom_call_target="tpu_custom_call" | custom-call | tf_op jit(solution)/shard_map/pallas_call | solution.py:224
  111.6 1.7 copy.24
  113.3 2.5 %convolution_bitcast_fusion = f32[4,384,96]{1,2,0:T(8,128)S(1)} fusion(f32[4,384,384]{2,1,0:T(8,128)S(1)} %bitcast.37, f32[384,96]{1,0:T(8,128)} %shard_map.60), kind=kOutput, calls=%fused_computation.3 | convolution fusion | flops 679477248 | bytes 3096576 | tf_op jit(solution)/shard_map/zim,ir->zmr/dot_general | solution.py:243
  115.8 0.3 copy.19
  116.0 3.0 %reshape.33 = f32[4,24,4,4,4,24]{5,4,3,2,1,0:T(4,128)} reshape(f32[4,384,96]{2,1,0:T(8,128)S(1)} %copy.19) | data formatting | bytes 1179648 | tf_op jit(solution)/shard_map/reshape | solution.py:244
  119.0 3.9 %copy.20 = f32[4,4,24,4,4,24]{5,4,3,2,1,0:T(4,128)S(1)} copy(f32[4,4,24,4,4,24]{5,0,3,1,2,4:T(4,128)} %bitcast.39) | data formatting | bytes 1179648 | tf_op jit(solution)/shard_map/transpose | solution.py:245
  122.9 4.5 %reshape.34.x_ref = f32[4,4,24,384]{3,2,1,0:T(8,128)} reshape(f32[4,4,24,4,4,24]{5,4,3,2,1,0:T(4,128)S(1)} %copy.20) | data formatting | bytes 1179648 | tf_op jit(solution)/shard_map/reshape | solution.py:245
  127.4 19.6 %shard_map.61 = f32[4,4,24,384]{3,2,1,0:T(8,128)} custom-call(f32[4,4,24,384]{3,2,1,0:T(8,128)} %reshape.34.x_ref), custom_call_target="tpu_custom_call" | custom-call | tf_op jit(solution)/shard_map/pallas_call | solution.py:168
  147.0 1.1 dot_general.29
  148.2 0.0 copy-start.3
  148.2 3.8 %fusion.8.x_ref = f32[2,4,4,12,384]{4,3,2,1,0:T(8,128)} fusion(f32[2,4,4,12,384]{4,3,2,1,0:T(8,128)S(1)} %dot_general.29, f32[384,384,1,1,1]{1,0,4,3,2:T(8,128)} %bitcast.40), kind=kOutput, calls=%fused_computation.7 | convolution fusion | flops 679477248 | bytes 1769472 | tf_op jit(solution)/shard_map/dot_general | solution.py:20
  152.0 0.0 copy-start.1
  152.0 25.6 %shard_map.62 = f32[2,4,4,12,384]{4,3,2,1,0:T(8,128)} custom-call(f32[2,4,4,12,384]{4,3,2,1,0:T(8,128)} %fusion.8.x_ref), custom_call_target="tpu_custom_call" | custom-call | tf_op jit(solution)/shard_map/pallas_call | solution.py:104
  177.6 2.0 %reshape.36.gram_ref = f32[384,384]{1,0:T(8,128)} reshape(f32[2,4,4,12,384]{4,3,2,1,0:T(8,128)} %shard_map.62) | data formatting | bytes 1179648 | tf_op jit(solution)/shard_map/reshape | solution.py:112
  179.7 0.0 copy-done.3
  179.7 0.8 copy.21.start_ref
  180.5 11.5 %shard_map.63 = f32[384,96]{1,0:T(8,128)} custom-call(f32[384,384]{1,0:T(8,128)} %reshape.36.gram_ref, f32[384,96]{1,0:T(8,128)} %copy.21.start_ref), custom_call_target="tpu_custom_call" | custom-call | tf_op jit(solution)/shard_map/pallas_call | solution.py:224
  192.0 1.7 copy.25
  193.7 0.0 copy-done.1
  193.7 0.2 copy.22
  193.9 2.2 %fusion.5 = f32[4,4,24,96]{3,2,1,0:T(8,128)} fusion(f32[4,4,24,384]{3,2,1,0:T(8,128)S(1)} %bitcast.42, f32[384,96]{1,0:T(8,128)} %shard_map.63), kind=kOutput, calls=%fused_computation.4 | convolution fusion | flops 169869312 | bytes 884736 | tf_op jit(solution)/shard_map/dot_general | solution.py:20
Async XLA Ops:
  60.3 3.3 %copy-start = (f32[4,4,96,384]{3,2,1,0:T(8,128)S(1)}, f32[4,4,96,384]{3,2,1,0:T(8,128)}, u32[]{:S(2)}) copy-start(f32[4,4,96,384]{3,2,1,0:T(8,128)} %shard_map.58) | copy-start | bytes 7077892
  69.7 29.5 %copy-start.2 = (f32[384,96]{0,1:T(8,128)S(1)}, f32[384,96]{0,1:T(8,128)}, u32[]{:S(2)}) copy-start(f32[384,96]{0,1:T(8,128)} %param.4) | copy-start | bytes 442372
  148.2 31.5 %copy-start.3 = (f32[384,96]{0,1:T(8,128)S(1)}, f32[384,96]{0,1:T(8,128)}, u32[]{:S(2)}) copy-start(f32[384,96]{0,1:T(8,128)} %param.5) | copy-start | bytes 442372
  152.0 41.7 %copy-start.1 = (f32[4,4,24,384]{3,2,1,0:T(8,128)S(1)}, f32[4,4,24,384]{3,2,1,0:T(8,128)}, u32[]{:S(2)}) copy-start(f32[4,4,24,384]{3,2,1,0:T(8,128)} %shard_map.61) | copy-start | bytes 1769476

commit v2 on v1

--- a/solution.py
+++ b/solution.py
@@ -10,6 +10,7 @@
 S = 16
 ITERS = 2
 PANEL = 16
+LANES = 128
 MESH = pl.DeviceIdType.MESH
 VMEM = pl.BlockSpec(memory_space=pltpu.VMEM)
 
@@ -211,7 +212,7 @@
     return jnp.concatenate(done, axis=0)
 
 
-def power_kernel(gram_ref, start_ref, out_ref):
+def power_general_kernel(gram_ref, start_ref, out_ref):
     current = start_ref[...]
     for turn in range(ITERS):
         images = dot_dims(gram_ref[...], current, 1, 0)
@@ -222,14 +223,14 @@
 
 def leading(gram, start):
     return pl.pallas_call(
-        power_kernel,
+        power_general_kernel,
         out_shape=jax.ShapeDtypeStruct(start.shape, jnp.float32),
         in_specs=[VMEM, VMEM],
         out_specs=VMEM,
     )(gram, start)
 
 
-def local(nx, ny, nz, species_field, start_first, start_second):
+def local_general(nx, ny, nz, species_field, start_first, start_second):
     axes, sizes = ("gz", "gy", "gx"), (nz, ny, nx)
     fibres = gather_fibres(species_field, nx)
     partial_gram = jnp.einsum("zic,zjc->ij", fibres, fibres, precision=exact_precision)
@@ -253,6 +254,221 @@
     return (factor_first, factor_second, core)
 
 
+def upper_blocks(count):
+    return [(a, b) for a in range(count) for b in range(a, count)]
+
+
+def add_gram(gram_ref, parts, contract, first):
+    for slot, (a, b) in enumerate(upper_blocks(len(parts))):
+        block = pl.ds(slot * LANES, LANES)
+        term = dot_dims(parts[a], parts[b], contract, contract)
+        gram_ref[block, :] = term if first else gram_ref[block, :] + term
+
+
+def times_gram(current, gram_ref):
+    count = current.shape[1] // LANES
+    sums = [None] * count
+    for slot, (a, b) in enumerate(upper_blocks(count)):
+        block = gram_ref[slot * LANES : (slot + 1) * LANES, :]
+        terms = [(b, a, 0)] if a == b else [(b, a, 0), (a, b, 1)]
+        for to, of, contract in terms:
+            term = dot_dims(current[:, of * LANES : (of + 1) * LANES], block, 1, contract)
+            sums[to] = term if sums[to] is None else sums[to] + term
+    return jnp.concatenate(sums, axis=1)
+
+
+def power_steps(gram_ref, current):
+    for turn in range(ITERS):
+        images = times_gram(current, gram_ref)
+        cross = dot_dims(images, images, 1, 1)
+        current = dot_dims(inverse_lower(cross), images, 1, 0)
+    return current
+
+
+def first_power_kernel(gram_ref, start_ref, out_ref):
+    out_ref[...] = power_steps(gram_ref, start_ref[...])
+
+
+def second_power_kernel(groups, cells, gram_ref, start_ref, rows_ref, out_ref, core_ref):
+    extent = start_ref.shape[1]
+    chunks = extent // LANES
+    true = lax.broadcasted_iota(jnp.int32, (extent, extent), 0)
+    held = lax.broadcasted_iota(jnp.int32, (extent, extent), 1)
+    shift = cells.bit_length() - 1
+    chunk = lax.shift_right_logical(held, LANES.bit_length() - 1)
+    group = lax.shift_right_logical(held & (LANES - 1), shift)
+    order = jnp.where(true == (group * chunks + chunk) * cells + (held & (cells - 1)), 1.0, 0.0)
+    current = power_steps(gram_ref, dot_dims(start_ref[...], order, 1, 0))
+    out_ref[...] = dot_dims(current, order, 1, 1)
+    core_ref[...] = dot_dims(rows_ref[...], current, 1, 1)
+
+
+def species_major(block, order):
+    high = block.astype(jnp.bfloat16)
+    left = block - high.astype(jnp.float32)
+    middle = left.astype(jnp.bfloat16)
+    low = (left - middle.astype(jnp.float32)).astype(jnp.bfloat16)
+    moved = [
+        lax.dot_general(part, order, (((1,), (0,)), ((), ())), preferred_element_type=jnp.float32)
+        for part in (high, middle, low)
+    ]
+    return (moved[0] + moved[1]) + moved[2]
+
+
+def first_kernel(n, x_ref, fibres_ref, gram_ref, packed, send_sems, recv_sems):
+    me = lax.axis_index("gx")
+    depth, rows, columns = x_ref.shape
+    span = n * LANES
+    cells = span // S
+    width = columns // n
+    peers = partners(n, me)
+    greet([{"gx": p} for p in peers])
+    source = lax.broadcasted_iota(jnp.int32, (span, span), 0)
+    target = lax.broadcasted_iota(jnp.int32, (span, span), 1)
+    species = lax.shift_right_logical(target, cells.bit_length() - 1)
+    order = jnp.where(source == (target & (cells - 1)) * S + species, 1.0, 0.0).astype(jnp.bfloat16)
+    copies = []
+    for level in range(depth):
+        for chunk in range(columns // span):
+            moved = species_major(x_ref[level, :, chunk * span : (chunk + 1) * span], order)
+            lanes = pl.ds(chunk * LANES, LANES)
+            for p in range(n):
+                packed[level, p, :, lanes] = moved[:, p * LANES : (p + 1) * LANES]
+        for turn, p in enumerate(peers):
+            sem = level * (n - 1) + turn
+            copies.append(
+                send(packed.at[level, p], fibres_ref.at[level, me], send_sems.at[sem], recv_sems.at[sem], {"gx": p})
+            )
+        fibres_ref[level, me] = packed[level, me]
+    for level in range(depth):
+        for copy in copies[level * (n - 1) : (level + 1) * (n - 1)]:
+            copy.wait()
+        whole = fibres_ref[level].reshape(n * rows, width)
+        parts = [whole[a : a + LANES] for a in range(0, n * rows, LANES)]
+        add_gram(gram_ref, parts, 1, level == 0)
+
+
+def first_stage(field, n):
+    depth, rows, columns = field.shape
+    width = columns // n
+    blocks = len(upper_blocks(n * rows // LANES))
+    count = depth * (n - 1)
+    return pl.pallas_call(
+        functools.partial(first_kernel, n),
+        out_shape=(
+            jax.ShapeDtypeStruct((depth, n, rows, width), jnp.float32),
+            jax.ShapeDtypeStruct((blocks * LANES, LANES), jnp.float32),
+        ),
+        in_specs=[VMEM],
+        out_specs=(VMEM, VMEM),
+        scratch_shapes=[
+            pltpu.VMEM((depth, n, rows, width), jnp.float32),
+            pltpu.SemaphoreType.DMA((count,)),
+            pltpu.SemaphoreType.DMA((count,)),
+        ],
+        compiler_params=pltpu.CompilerParams(collective_id=0, has_side_effects=True),
+    )(field)
+
+
+def second_kernel(n, cells, factor_ref, fibres_ref, rows_ref, gram_ref, packed, land, send_sems, recv_sems):
+    me = lax.axis_index("gy")
+    depth, ranks, width = packed.shape[0], packed.shape[2], packed.shape[3]
+    peers = partners(n, me)
+    greet([{"gy": p} for p in peers])
+    copies = []
+    for level in range(depth):
+        whole = fibres_ref[level].reshape(factor_ref.shape[1], width)
+        projected = dot_dims(factor_ref[...], whole, 1, 0)
+        packed[level] = projected.reshape(n, ranks, width)
+        for turn, p in enumerate(peers):
+            sem = level * (n - 1) + turn
+            copies.append(
+                send(packed.at[level, p], land.at[me, level], send_sems.at[sem], recv_sems.at[sem], {"gy": p})
+            )
+        land[me, level] = packed[level, me]
+    lane_group = lax.shift_right_logical(
+        lax.broadcasted_iota(jnp.int32, (ranks, LANES), 1), cells.bit_length() - 1
+    )
+    for level in range(depth):
+        for copy in copies[level * (n - 1) : (level + 1) * (n - 1)]:
+            copy.wait()
+        for chunk in range(width // LANES):
+            lanes = pl.ds(chunk * LANES, LANES)
+            pieces = [land[t, level, :, lanes] for t in range(n)]
+            for s in range(n):
+                merged = pieces[s]
+                for t in range(n):
+                    if t != s:
+                        turned = pltpu.roll(pieces[t], cells * ((t - s) % n), 1)
+                        merged = jnp.where(lane_group == t, turned, merged)
+                rows_ref[s, level, :, lanes] = merged
+        whole = rows_ref[:, level].reshape(n * ranks, width)
+        parts = [whole[:, a : a + LANES] for a in range(0, width, LANES)]
+        add_gram(gram_ref, parts, 0, level == 0)
+
+
+def second_stage(factor, fibres, n, cells):
+    depth, _, _, width = fibres.shape
+    ranks = factor.shape[0] // n
+    blocks = len(upper_blocks(width // LANES))
+    count = depth * (n - 1)
+    return pl.pallas_call(
+        functools.partial(second_kernel, n, cells),
+        out_shape=(
+            jax.ShapeDtypeStruct((n, depth, ranks, width), jnp.float32),
+            jax.ShapeDtypeStruct((blocks * LANES, LANES), jnp.float32),
+        ),
+        in_specs=[VMEM, VMEM],
+        out_specs=(VMEM, VMEM),
+        scratch_shapes=[
+            pltpu.VMEM((depth, n, ranks, width), jnp.float32),
+            pltpu.VMEM((n, depth, ranks, width), jnp.float32),
+            pltpu.SemaphoreType.DMA((count,)),
+            pltpu.SemaphoreType.DMA((count,)),
+        ],
+        compiler_params=pltpu.CompilerParams(collective_id=1, has_side_effects=True),
+    )(factor, fibres)
+
+
+def local(nx, ny, nz, species_field, start_first, start_second):
+    depth, rows, columns = species_field.shape
+    rank, extent = start_first.shape[1], start_second.shape[0]
+    species, ranks = S // nx, rank // ny
+    cells = LANES // species
+    fits = (
+        columns % (nx * LANES) == 0
+        and columns // nx == extent
+        and species == ny
+        and extent % LANES == 0
+        and nx * rows % LANES == 0
+        and ranks % 8 == 0
+    )
+    if not fits:
+        return local_general(nx, ny, nz, species_field, start_first, start_second)
+    axes, sizes = ("gz", "gy", "gx"), (nz, ny, nx)
+    fibres, partial_first = first_stage(species_field, nx)
+    gram_first = all_reduce(partial_first, axes, sizes, 2)
+    factor_first = pl.pallas_call(
+        first_power_kernel,
+        out_shape=jax.ShapeDtypeStruct((rank, nx * rows), jnp.float32),
+        in_specs=[VMEM, VMEM],
+        out_specs=VMEM,
+    )(gram_first, start_first.T)
+    rows_second, partial_second = second_stage(factor_first, fibres, ny, cells)
+    gram_second = all_reduce(partial_second, axes, sizes, 3)
+    rows_second = rows_second.reshape(species * depth * ranks, extent)
+    factor_second, core = pl.pallas_call(
+        functools.partial(second_power_kernel, ny, cells),
+        out_shape=(
+            jax.ShapeDtypeStruct((rank, extent), jnp.float32),
+            jax.ShapeDtypeStruct((rows_second.shape[0], rank), jnp.float32),
+        ),
+        in_specs=[VMEM, VMEM, VMEM],
+        out_specs=(VMEM, VMEM),
+    )(gram_second, start_second.T, rows_second)
+    return (factor_first.T, factor_second.T, core.reshape(species, depth, ranks, rank))
+
+
 def solution(mesh):
     return jax.shard_map(
         functools.partial(local, mesh.shape["gx"], mesh.shape["gy"], mesh.shape["gz"]),

time: 197 us -> 144 us (0.73)
  local copies, waits for them, and re-layouts: 25.4 us -> 0 us
  matrix products: 14.6 us -> 0 us
  Pallas kernels: 156 us -> 143 us
    reshape x5 -> x0, local copies, waits for them, and re-layouts: 14.8 us -> none  [the longest x1 4.46 us: local(): blocks.transpose(4, 2, 1, 3, 0, 5)]
    dot_general x4 -> x0, matrix products: 14.6 us -> none  [the longest x2 6.07 us: dot_dims(): lax.dot_general(a, b, (((contract_a,), (contract_b,)), ((), ())), precisi...]
    pallas_call x2, Pallas kernels: 53.1 us -> 43.5 us  [all_reduce(): pl.pallas_call(functools.partial(all_reduce_kernel, axes, sizes, splits),...]
    unnamed x12 -> x0, local copies, waits for them, and re-layouts: 5.06 us -> none
    transpose x1 -> x0, local copies, waits for them, and re-layouts: 3.91 us -> none  [local(): blocks.transpose(4, 2, 1, 3, 0, 5)]
    pallas_call x4, Pallas kernels: 102 us -> 99.9 us  [the longest x1 61.6 us: first_stage(): pl.pallas_call(functools.partial(first_kernel, n), out_shape=(jax.ShapeDt...]
where the time goes in v2:
time: 144 us
  Pallas kernels  143 us (99%)
    pallas_call x1, Pallas kernels, first_stage(): pl.pallas_call(functools.partial(first_kernel, n), out_shape=(jax.ShapeDt...  61.6 us
    pallas_call x2, Pallas kernels, all_reduce(): pl.pallas_call(functools.partial(all_reduce_kernel, axes, sizes, splits),...  43.5 us
    pallas_call x1, Pallas kernels, second_stage(): pl.pallas_call(functools.partial(second_kernel, n, cells), out_shape=(jax...  13.7 us
    pallas_call x1, Pallas kernels, local(): pl.pallas_call(functools.partial(second_power_kernel, ny, cells), out_sha...  13.2 us
    pallas_call x1, Pallas kernels, local(): pl.pallas_call(first_power_kernel, out_shape=jax.ShapeDtypeStruct((rank,...  11.5 us

profile of v2, /device:TPU:0, one launch (start us, length us, event | category | flops | bytes accessed | tf_op | source)
XLA Modules:
  0.0 144.1 jit_solution(1173537164229132491)
XLA Ops:
  0.6 61.6 %shard_map.58 = (f32[4,4,96,384]{3,2,1,0:T(8,128)}, f32[768,128]{1,0:T(8,128)}) custom-call(f32[4,96,1536]{2,1,0:T(8,128)} %x_ref.1), custom_call_target="tpu_custom_call" | custom-call | tf_op jit(solution)/shard_map/pallas_call | solution.py:356
  62.2 22.7 %shard_map.59 = f32[2,4,4,24,128]{4,3,2,1,0:T(8,128)} custom-call(f32[2,4,4,24,128]{4,3,2,1,0:T(8,128)} %bitcast.15), custom_call_target="tpu_custom_call" | custom-call | tf_op jit(solution)/shard_map/pallas_call | solution.py:105
  84.9 11.5 %shard_map.60.factor_ref = f32[96,384]{1,0:T(8,128)} custom-call(f32[768,128]{1,0:T(8,128)} %bitcast.11, f32[96,384]{1,0:T(8,128)} %bitcast.17), custom_call_target="tpu_custom_call" | custom-call | tf_op jit(solution)/shard_map/pallas_call | solution.py:451
  96.4 13.7 %shard_map.61 = (f32[4,4,24,384]{3,2,1,0:T(8,128)}, f32[768,128]{1,0:T(8,128)}) custom-call(f32[96,384]{1,0:T(8,128)} %shard_map.60.factor_ref, f32[4,4,96,384]{3,2,1,0:T(8,128)} %get-tuple-element.10.fibres_ref), custom_call_target="tpu_custom_call" | custom-call | tf_op jit(solution)/shard_map/pallas_call | solution.py:415
  110.1 20.8 %shard_map.62 = f32[2,4,4,24,128]{4,3,2,1,0:T(8,128)} custom-call(f32[2,4,4,24,128]{4,3,2,1,0:T(8,128)} %bitcast.14), custom_call_target="tpu_custom_call" | custom-call | tf_op jit(solution)/shard_map/pallas_call | solution.py:105
  130.9 13.2 %shard_map.63 = (f32[96,384]{1,0:T(8,128)}, f32[384,96]{1,0:T(8,128)}) custom-call(f32[768,128]{1,0:T(8,128)} %bitcast.10, f32[96,384]{1,0:T(8,128)} %bitcast.16, f32[384,384]{1,0:T(8,128)} %bitcast.13), custom_call_target="tpu_custom_call" | custom-call | tf_op jit(solution)/shard_map/pallas_call | solution.py:460

commit v3 on v2

--- a/solution.py
+++ b/solution.py
@@ -39,21 +39,31 @@
     return copy
 
 
-def greet(targets):
+def say_hello(targets):
     barrier = pltpu.get_barrier_semaphore()
     for target in targets:
         pl.semaphore_signal(barrier, inc=1, device_id=target, device_id_type=MESH)
-    pl.semaphore_wait(barrier, len(targets))
-
-
-def all_reduce_kernel(axes, sizes, splits, x_ref, o_ref, *scratch):
+
+
+def hear_hello(targets):
+    pl.semaphore_wait(pltpu.get_barrier_semaphore(), len(targets))
+
+
+def greet(targets):
+    say_hello(targets)
+    hear_hello(targets)
+
+
+def axis_peers(axes, sizes):
+    return [{axis: p} for axis, n in zip(axes, sizes) for p in partners(n, lax.axis_index(axis))]
+
+
+def reduce_blocks(axes, sizes, splits, x_ref, o_ref, scratch):
     levels = len(axes)
     landing, totals = scratch[:levels], scratch[levels : 2 * levels - 1]
     send_sems, recv_sems = scratch[2 * levels - 1 :]
     me = [lax.axis_index(axis) for axis in axes]
     peers = [partners(n, m) for n, m in zip(sizes, me)]
-    greet([{axis: p} for axis, ps in zip(axes, peers) for p in ps])
-
     spot = [m if split > 1 else 0 for m, split in zip(me, splits)]
     sem = 0
     held = x_ref
@@ -89,27 +99,36 @@
             copy.wait()
 
 
-def all_reduce(x, axes, sizes, collective_id):
-    rows, columns = x.shape
+def all_reduce_kernel(axes, sizes, splits, x_ref, o_ref, *scratch):
+    greet(axis_peers(axes, sizes))
+    reduce_blocks(axes, sizes, splits, x_ref, o_ref, scratch)
+
+
+def reduce_plan(rows, columns, sizes):
     splits = []
     for n in sizes:
         splits.append(n if rows % n == 0 else 1)
         rows //= splits[-1]
-    blocked = x.reshape(*splits, rows, columns)
-    landing = [
+    scratch = [
         pltpu.VMEM((n, *splits[level + 1 :], rows, columns), jnp.float32)
         for level, n in enumerate(sizes)
     ]
-    totals = [pltpu.VMEM((*splits[level + 1 :], rows, columns), jnp.float32) for level in range(len(sizes) - 1)]
+    scratch += [pltpu.VMEM((*splits[level + 1 :], rows, columns), jnp.float32) for level in range(len(sizes) - 1)]
     count = sum(n - 1 for n in sizes) + sum(n - 1 for n, split in zip(sizes, splits) if split > 1)
+    scratch += [pltpu.SemaphoreType.DMA((count,)), pltpu.SemaphoreType.DMA((count,))]
+    return splits, (*splits, rows, columns), scratch
+
+
+def all_reduce(x, axes, sizes, collective_id):
+    splits, blocked, scratch = reduce_plan(*x.shape, sizes)
     out = pl.pallas_call(
         functools.partial(all_reduce_kernel, axes, sizes, splits),
-        out_shape=jax.ShapeDtypeStruct(blocked.shape, jnp.float32),
+        out_shape=jax.ShapeDtypeStruct(blocked, jnp.float32),
         in_specs=[VMEM],
         out_specs=VMEM,
-        scratch_shapes=landing + totals + [pltpu.SemaphoreType.DMA((count,)), pltpu.SemaphoreType.DMA((count,))],
+        scratch_shapes=scratch,
         compiler_params=pltpu.CompilerParams(collective_id=collective_id, has_side_effects=True),
-    )(blocked)
+    )(x.reshape(blocked))
     return out.reshape(x.shape)
 
 
@@ -285,10 +304,6 @@
     return current
 
 
-def first_power_kernel(gram_ref, start_ref, out_ref):
-    out_ref[...] = power_steps(gram_ref, start_ref[...])
-
-
 def second_power_kernel(groups, cells, gram_ref, start_ref, rows_ref, out_ref, core_ref):
     extent = start_ref.shape[1]
     chunks = extent // LANES
@@ -315,71 +330,56 @@
     return (moved[0] + moved[1]) + moved[2]
 
 
-def first_kernel(n, x_ref, fibres_ref, gram_ref, packed, send_sems, recv_sems):
+def first_exchange(n, targets, x_ref, field, fibres, gram, packed, load_sems, send_sems, recv_sems):
     me = lax.axis_index("gx")
-    depth, rows, columns = x_ref.shape
+    depth, rows, columns = field.shape
     span = n * LANES
     cells = span // S
     width = columns // n
+    loads = [pltpu.make_async_copy(x_ref.at[z], field.at[z], load_sems.at[z]) for z in range(depth)]
+    for load in loads:
+        load.start()
+    say_hello(targets)
     peers = partners(n, me)
-    greet([{"gx": p} for p in peers])
     source = lax.broadcasted_iota(jnp.int32, (span, span), 0)
     target = lax.broadcasted_iota(jnp.int32, (span, span), 1)
     species = lax.shift_right_logical(target, cells.bit_length() - 1)
     order = jnp.where(source == (target & (cells - 1)) * S + species, 1.0, 0.0).astype(jnp.bfloat16)
     copies = []
     for level in range(depth):
+        loads[level].wait()
         for chunk in range(columns // span):
-            moved = species_major(x_ref[level, :, chunk * span : (chunk + 1) * span], order)
+            moved = species_major(field[level, :, chunk * span : (chunk + 1) * span], order)
             lanes = pl.ds(chunk * LANES, LANES)
             for p in range(n):
                 packed[level, p, :, lanes] = moved[:, p * LANES : (p + 1) * LANES]
-        for turn, p in enumerate(peers):
+        if level == 0:
+            hear_hello(targets)
+        turns = list(enumerate(peers))
+        if level > 0:
+            turns = turns[-1:] + turns[:-1]
+        for turn, p in turns:
             sem = level * (n - 1) + turn
             copies.append(
-                send(packed.at[level, p], fibres_ref.at[level, me], send_sems.at[sem], recv_sems.at[sem], {"gx": p})
+                send(packed.at[level, p], fibres.at[level, me], send_sems.at[sem], recv_sems.at[sem], {"gx": p})
             )
-        fibres_ref[level, me] = packed[level, me]
+        fibres[level, me] = packed[level, me]
     for level in range(depth):
         for copy in copies[level * (n - 1) : (level + 1) * (n - 1)]:
             copy.wait()
-        whole = fibres_ref[level].reshape(n * rows, width)
+        whole = fibres[level].reshape(n * rows, width)
         parts = [whole[a : a + LANES] for a in range(0, n * rows, LANES)]
-        add_gram(gram_ref, parts, 1, level == 0)
-
-
-def first_stage(field, n):
-    depth, rows, columns = field.shape
-    width = columns // n
-    blocks = len(upper_blocks(n * rows // LANES))
-    count = depth * (n - 1)
-    return pl.pallas_call(
-        functools.partial(first_kernel, n),
-        out_shape=(
-            jax.ShapeDtypeStruct((depth, n, rows, width), jnp.float32),
-            jax.ShapeDtypeStruct((blocks * LANES, LANES), jnp.float32),
-        ),
-        in_specs=[VMEM],
-        out_specs=(VMEM, VMEM),
-        scratch_shapes=[
-            pltpu.VMEM((depth, n, rows, width), jnp.float32),
-            pltpu.SemaphoreType.DMA((count,)),
-            pltpu.SemaphoreType.DMA((count,)),
-        ],
-        compiler_params=pltpu.CompilerParams(collective_id=0, has_side_effects=True),
-    )(field)
-
-
-def second_kernel(n, cells, factor_ref, fibres_ref, rows_ref, gram_ref, packed, land, send_sems, recv_sems):
+        add_gram(gram, parts, 1, level == 0)
+
+
+def second_exchange(n, cells, factor, fibres, rows_ref, gram, packed, land, send_sems, recv_sems):
     me = lax.axis_index("gy")
     depth, ranks, width = packed.shape[0], packed.shape[2], packed.shape[3]
     peers = partners(n, me)
-    greet([{"gy": p} for p in peers])
     copies = []
     for level in range(depth):
-        whole = fibres_ref[level].reshape(factor_ref.shape[1], width)
-        projected = dot_dims(factor_ref[...], whole, 1, 0)
-        packed[level] = projected.reshape(n, ranks, width)
+        whole = fibres[level].reshape(factor.shape[1], width)
+        packed[level] = dot_dims(factor, whole, 1, 0).reshape(n, ranks, width)
         for turn, p in enumerate(peers):
             sem = level * (n - 1) + turn
             copies.append(
@@ -404,30 +404,67 @@
                 rows_ref[s, level, :, lanes] = merged
         whole = rows_ref[:, level].reshape(n * ranks, width)
         parts = [whole[:, a : a + LANES] for a in range(0, width, LANES)]
-        add_gram(gram_ref, parts, 0, level == 0)
-
-
-def second_stage(factor, fibres, n, cells):
-    depth, _, _, width = fibres.shape
-    ranks = factor.shape[0] // n
-    blocks = len(upper_blocks(width // LANES))
-    count = depth * (n - 1)
+        add_gram(gram, parts, 0, level == 0)
+
+
+def stages_kernel(axes, sizes, cells, splits, x_ref, start_ref, factor_ref, rows_ref, gram_ref, *scratch):
+    ny, nx = sizes[1], sizes[2]
+    targets = axis_peers(axes, sizes)
+    gram, field, fibres, packed, load_sems, send_first, recv_first = scratch[:7]
+    packed_second, land, send_second, recv_second = scratch[7:11]
+    half = (len(scratch) - 11) // 2
+    reduces = scratch[11 : 11 + half], scratch[11 + half :]
+
+    def reduced(reduce_scratch, into):
+        held, total = reduce_scratch[0], reduce_scratch[1]
+        held[...] = gram[...].reshape(held.shape)
+        reduce_blocks(axes, sizes, splits, held, total, reduce_scratch[2:])
+        into[...] = total[...].reshape(into.shape)
+
+    first_exchange(nx, targets, x_ref, field, fibres, gram, packed, load_sems, send_first, recv_first)
+    reduced(reduces[0], gram)
+    factor = power_steps(gram, start_ref[...])
+    factor_ref[...] = factor
+    second_exchange(ny, cells, factor, fibres, rows_ref, gram, packed_second, land, send_second, recv_second)
+    reduced(reduces[1], gram_ref)
+
+
+def stages(field, start, axes, sizes, cells):
+    ny, nx = sizes[1], sizes[2]
+    depth, rows, columns = field.shape
+    rank, extent = start.shape
+    width = columns // nx
+    ranks = rank // ny
+    gram_shape = (len(upper_blocks(extent // LANES)) * LANES, LANES)
+    splits, blocked, reduce_scratch = reduce_plan(*gram_shape, sizes)
+    reduce_scratch = [pltpu.VMEM(blocked, jnp.float32)] * 2 + reduce_scratch
+    first, second = depth * (nx - 1), depth * (ny - 1)
     return pl.pallas_call(
-        functools.partial(second_kernel, n, cells),
+        functools.partial(stages_kernel, axes, sizes, cells, splits),
         out_shape=(
-            jax.ShapeDtypeStruct((n, depth, ranks, width), jnp.float32),
-            jax.ShapeDtypeStruct((blocks * LANES, LANES), jnp.float32),
+            jax.ShapeDtypeStruct((rank, extent), jnp.float32),
+            jax.ShapeDtypeStruct((ny, depth, ranks, width), jnp.float32),
+            jax.ShapeDtypeStruct(gram_shape, jnp.float32),
         ),
-        in_specs=[VMEM, VMEM],
-        out_specs=(VMEM, VMEM),
+        in_specs=[pl.BlockSpec(memory_space=pl.ANY), VMEM],
+        out_specs=(VMEM, VMEM, VMEM),
         scratch_shapes=[
-            pltpu.VMEM((depth, n, ranks, width), jnp.float32),
-            pltpu.VMEM((n, depth, ranks, width), jnp.float32),
-            pltpu.SemaphoreType.DMA((count,)),
-            pltpu.SemaphoreType.DMA((count,)),
+            pltpu.VMEM(gram_shape, jnp.float32),
+            pltpu.VMEM((depth, rows, columns), jnp.float32),
+            pltpu.VMEM((depth, nx, rows, width), jnp.float32),
+            pltpu.VMEM((depth, nx, rows, width), jnp.float32),
+            pltpu.SemaphoreType.DMA((depth,)),
+            pltpu.SemaphoreType.DMA((first,)),
+            pltpu.SemaphoreType.DMA((first,)),
+            pltpu.VMEM((depth, ny, ranks, width), jnp.float32),
+            pltpu.VMEM((ny, depth, ranks, width), jnp.float32),
+            pltpu.SemaphoreType.DMA((second,)),
+            pltpu.SemaphoreType.DMA((second,)),
+            *reduce_scratch,
+            *reduce_scratch,
         ],
-        compiler_params=pltpu.CompilerParams(collective_id=1, has_side_effects=True),
-    )(factor, fibres)
+        compiler_params=pltpu.CompilerParams(collective_id=0, has_side_effects=True),
+    )(field, start)
 
 
 def local(nx, ny, nz, species_field, start_first, start_second):
@@ -438,6 +475,7 @@
     fits = (
         columns % (nx * LANES) == 0
         and columns // nx == extent
+        and nx * rows == extent
         and species == ny
         and extent % LANES == 0
         and nx * rows % LANES == 0
@@ -446,16 +484,7 @@
     if not fits:
         return local_general(nx, ny, nz, species_field, start_first, start_second)
     axes, sizes = ("gz", "gy", "gx"), (nz, ny, nx)
-    fibres, partial_first = first_stage(species_field, nx)
-    gram_first = all_reduce(partial_first, axes, sizes, 2)
-    factor_first = pl.pallas_call(
-        first_power_kernel,
-        out_shape=jax.ShapeDtypeStruct((rank, nx * rows), jnp.float32),
-        in_specs=[VMEM, VMEM],
-        out_specs=VMEM,
-    )(gram_first, start_first.T)
-    rows_second, partial_second = second_stage(factor_first, fibres, ny, cells)
-    gram_second = all_reduce(partial_second, axes, sizes, 3)
+    factor_first, rows_second, gram_second = stages(species_field, start_first.T, axes, sizes, cells)
     rows_second = rows_second.reshape(species * depth * ranks, extent)
     factor_second, core = pl.pallas_call(
         functools.partial(second_power_kernel, ny, cells),

time: 144 us -> 132 us (0.917)
  Pallas kernels: 143 us -> 130 us
  local copies, waits for them, and re-layouts: 0 us -> 1.58 us
    pallas_call x5 -> x1, Pallas kernels: 130 us -> 117 us  [stages(): pl.pallas_call(functools.partial(stages_kernel, axes, sizes, cells, split...]
    unnamed x0 -> x1, local copies, waits for them, and re-layouts: none -> 1.58 us
where the time goes in v3:
time: 132 us
  Pallas kernels  130 us (98%)
  local copies, waits for them, and re-layouts  1.58 us (1%)
    pallas_call x1, Pallas kernels, stages(): pl.pallas_call(functools.partial(stages_kernel, axes, sizes, cells, split...  117 us
    pallas_call x1, Pallas kernels, local(): pl.pallas_call(functools.partial(second_power_kernel, ny, cells), out_sha...  13.2 us

profile of v3, /device:TPU:0, one launch (start us, length us, event | category | flops | bytes accessed | tf_op | source)
XLA Modules:
  0.0 132.0 jit_solution(18033731849363578292)
XLA Ops:
  0.6 116.6 %shard_map.58 = (f32[96,384]{1,0:T(8,128)}, f32[4,4,24,384]{3,2,1,0:T(8,128)}, f32[768,128]{1,0:T(8,128)}) custom-call(f32[4,96,1536]{2,1,0:T(8,128)} %x_ref.1, f32[96,384]{1,0:T(8,128)} %bitcast.7), custom_call_target="tpu_custom_call" | custom-call | tf_op jit(solution)/shard_map/pallas_call | solution.py:442
  117.3 13.2 %shard_map.59 = (f32[96,384]{1,0:T(8,128)}, f32[384,96]{1,0:T(8,128)}) custom-call(f32[768,128]{1,0:T(8,128)} %get-tuple-element.9.gram_ref, f32[96,384]{1,0:T(8,128)} %bitcast.8, f32[384,384]{1,0:T(8,128)} %bitcast.6), custom_call_target="tpu_custom_call" | custom-call | tf_op jit(solution)/shard_map/pallas_call | solution.py:489
  130.4 1.6 %copy.7 = f32[384,96]{0,1:T(8,128)} copy(f32[384,96]{0,1:T(8,128)} %bitcast.9) | data formatting | bytes 294912
